TPU v7x, 32 devices: a whole 2x2x4 slice. The times are simulated.
32 devices in a mesh: sub: 32 (over z, y, x, core).
Axes of the slice: x: 2, y: 2, z: 4, core: 2. Of those that a mesh axis runs over, the one named last changes fastest.
Arguments:
- images: float32 [2, 4, 512, 4096], P(None, None, 'sub'), may hold values from -6 to 6
- anchors: int32 [128], P('sub'), may hold values from 0 to 4095, as said below
- patches: int32 [128], P('sub'), may hold values from 0 to 31
- coeffs: float32 [4, 45, 32], P(None, None, 'sub'), may hold values from -1.2 to 1.2
- zbasis: float32 [45, 4096], replicated, may hold values from -4 to 4
Outputs:
- new_coeffs: float32 [4, 45, 32], P(None, None, 'sub')
- last_gradient: float32 [4, 45, 32], P(None, None, 'sub')
Inputs may be any that keep to these rules, and one draw needn't show every extreme that they name: `anchors`: the first column of subfield s lies among the 128 columns that begin at 128 * (s // 4).
All inputs are finite; a program needn't handle non-finite values.
Results may differ from a plain program's by a relative error of at most 0.0003.
Values sent between devices are 32-bit elements; how exact they have to be, the bound alone decides.
A program may use at most 128 MiB of HBM per device.

v0:
```python
import math
import jax
import jax.numpy as jnp
from jax import lax
from jax.sharding import PartitionSpec as P

SUB = 128
CH = 2
TR = 4
ITERS = 2
PUP = 64
GAMMA = 0.01
STEP_SIZE = 0.05


def from_behind(block, axis, distance):
    devices = range(lax.axis_size(axis))
    route = [(i - distance, i) for i in devices if i - distance in devices]
    return lax.ppermute(block, axis, route)


def taper(length):
    cells = jnp.arange(length, dtype=jnp.float32)
    return 0.5 - 0.5 * jnp.cos(2.0 * math.pi * (cells + 0.5) / length)


def aperture(width):
    centred = jnp.arange(width, dtype=jnp.float32) - width / 2 + 0.5
    radius = centred[:, None] ** 2 + centred[None, :] ** 2
    return (radius <= (width / 2) ** 2).astype(jnp.float32)


def dft_tables(length):
    indices = jnp.arange(length, dtype=jnp.int32)
    product_mod = indices[:, None] * indices[None, :] % length
    angles = 2.0 * math.pi / length * product_mod.astype(jnp.float32)
    return (jnp.cos(angles), -jnp.sin(angles))


def complex_dft(real_part, imag_part, left_table, right_table):
    highest = lax.Precision.HIGHEST
    right_real, right_imag = right_table
    left_real, left_imag = left_table
    half_real = jnp.einsum("...ab,kb->...ak", real_part, right_real, precision=highest)
    half_imag = jnp.einsum("...ab,kb->...ak", real_part, right_imag, precision=highest)
    if imag_part is not None:
        half_real = half_real - jnp.einsum(
            "...ab,kb->...ak", imag_part, right_imag, precision=highest
        )
        half_imag = half_imag + jnp.einsum(
            "...ab,kb->...ak", imag_part, right_real, precision=highest
        )
    out_real = jnp.einsum("ja,...ak->...jk", left_real, half_real, precision=highest) - jnp.einsum(
        "ja,...ak->...jk", left_imag, half_imag, precision=highest
    )
    out_imag = jnp.einsum("ja,...ak->...jk", left_real, half_imag, precision=highest) + jnp.einsum(
        "ja,...ak->...jk", left_imag, half_real, precision=highest
    )
    return (out_real, out_imag)


def on_device(images, anchors, patches, coeffs, zbasis):
    highest = lax.Precision.HIGHEST
    devices = lax.axis_size("sub")
    device_index = lax.axis_index("sub")
    strip_width = images.shape[3] // devices
    reach = SUB // strip_width
    column_strip = lax.all_to_all(images, "sub", split_axis=3, concat_axis=2, tiled=True)
    strip_list = [column_strip]
    for step_right in range(1, reach + 1):
        strip_list.append(from_behind(column_strip, "sub", -step_right))
    widened = jnp.concatenate(strip_list, axis=3)
    offsets = anchors - device_index * strip_width
    subfield_list = []
    for row_tile in range(TR):
        strip_rows = widened[:, :, row_tile * SUB : (row_tile + 1) * SUB, :]
        subfield_list.append(lax.dynamic_slice_in_dim(strip_rows, offsets[row_tile], SUB, 3))
    window_two = taper(SUB)[:, None] * taper(SUB)[None, :]
    subfields = jnp.stack(subfield_list, axis=2) * window_two
    full_real, full_imag = dft_tables(SUB)
    full_table = (full_real, full_imag)
    pupil_table = (full_real[:, :PUP], full_imag[:, :PUP])
    data_real, data_imag = complex_dft(subfields, None, full_table, full_table)
    power_sum = jnp.sum(data_real * data_real + data_imag * data_imag, axis=1)
    pupil_mask = aperture(PUP)
    pupil_area = jnp.sum(pupil_mask)
    ratios = 1.0 / (1.0 + 0.25 * jnp.arange(CH, dtype=jnp.float32))
    owned_count = coeffs.shape[2]
    total_patches = owned_count * devices
    selector = (patches[None, :] == jnp.arange(total_patches, dtype=jnp.int32)[:, None]).astype(
        jnp.float32
    )

    def objective(chosen):
        phases = jnp.einsum("fms,mq->fsq", chosen, zbasis, precision=highest)
        phases = phases.reshape(phases.shape[:2] + (PUP, PUP))
        scaled = ratios[:, None, None, None, None] * phases[None]
        pupil_real = pupil_mask * jnp.cos(scaled)
        pupil_imag = pupil_mask * jnp.sin(scaled)
        field_real, field_imag = complex_dft(pupil_real, pupil_imag, pupil_table, pupil_table)
        psf_values = (field_real * field_real + field_imag * field_imag) / (SUB * SUB * pupil_area)
        otf_real, otf_imag = complex_dft(psf_values, None, full_table, full_table)
        cross_real = jnp.sum(data_real * otf_real + data_imag * otf_imag, axis=1)
        cross_imag = jnp.sum(data_imag * otf_real - data_real * otf_imag, axis=1)
        denominator = jnp.sum(otf_real * otf_real + otf_imag * otf_imag, axis=1) + GAMMA
        return (
            jnp.sum(power_sum - (cross_real * cross_real + cross_imag * cross_imag) / denominator)
            / SUB**4
        )

    current = coeffs
    gradient = jnp.zeros_like(coeffs)
    for iteration in range(ITERS):
        gathered = lax.all_gather(current, "sub", axis=2, tiled=True)
        chosen = jnp.einsum("fmp,ps->fms", gathered, selector, precision=highest)
        loss_value, pullback = jax.vjp(objective, chosen)
        (slopes,) = pullback(jnp.ones_like(loss_value))
        spread = jnp.einsum("fms,ps->fmp", slopes, selector, precision=highest)
        gradient = lax.psum_scatter(spread, "sub", scatter_dimension=2, tiled=True)
        current = current - STEP_SIZE * gradient
    return (current, gradient)


def solution(mesh):
    return jax.shard_map(
        on_device,
        mesh=mesh,
        in_specs=(P(None, None, "sub", None), P("sub"), P("sub"), P(None, None, "sub"), P()),
        out_specs=(P(None, None, "sub"), P(None, None, "sub")),
        check_vma=False,
    )
```

profile of v0, /device:TPU:10, one launch (start us, length us, event | category | flops | bytes accessed | tf_op | source)
XLA Modules:
  0.0 485.6 jit_solution(7883281226299236298)
XLA Ops:
  0.6 13.1 %copy.172 = f32[2,4,16,4096]{2,1,0,3:T(4,128)} copy(f32[2,4,16,4096]{3,2,1,0:T(8,128)} %param.5) | data formatting | bytes 4194304 | tf_op args[0]
  13.7 16.4 %reshape.149 = f32[32,1,16384]{2,1,0:T(1,128)} reshape(f32[4096,2,4,16]{3,2,1,0:T(4,128)} %bitcast.273) | data formatting | bytes 4194304
  30.1 6.1 %all-to-all-start = ((f32[32,1,16384]{2,1,0:T(1,128)}), f32[32,1,16384]{2,1,0:T(1,128)}, u32[]{:S(2)}, u32[]{:S(2)}) async-start(f32[32,1,16384]{2,1,0:T(1,128)} %reshape.149), calls=%async_computation | async-start | bytes 4194304 | tf_op jit(solution)/shard_map/all_to_all | solution.py:68
  36.3 71.0 %all_gather.6 = f32[4,45,32]{1,0,2:T(4,128)S(1)} all-gather(f32[4,45,1]{1,0,2:T(4,128)S(1)} %bitcast.277), channel_id=1, replica_groups=mesh['sub'=32] {'sub'}, dimensions={2}, use_global_device_ids=true | all-gather | bytes 23760 | tf_op jit(solution)/shard_map/all_gather | solution.py:114
  111.0 4.4 fusion.52
  115.4 4.4 fusion.54
  119.8 4.6 fusion.63
  124.3 4.4 fusion.60
  148.8 8.7 %reduce.6 = f32[32,16384]{1,0:T(8,128)} reduce(f32[32,1,16384]{2,1,0:T(1,128)} %all-to-all-done, f32[]{:T(128)} %broadcast.349), dimensions={1}, to_apply=%all_to_all.13.reduce_sub_computation | reduce | bytes 4194308 | tf_op jit(solution)/shard_map/all_to_all | solution.py:68
  157.6 14.7 %reshape.150 = f32[4096,2,4,16]{3,2,1,0:T(4,128)} reshape(f32[32,16384]{1,0:T(8,128)} %reduce.6) | data formatting | bytes 4194304
  172.3 13.7 %copy.286 = f32[2,4,16,32,128]{4,2,3,1,0:T(8,128)} copy(f32[2,4,16,32,128]{2,1,0,4,3:T(4,128)} %bitcast.272) | data formatting | bytes 4194304 | tf_op jit(solution)/shard_map/all_to_all | solution.py:68
  245.2 4.9 %add_divide_fusion.2 = f32[2,4,4,128,128]{4,3,2,1,0:T(8,128)} fusion(f32[2,4,4,128,128]{4,3,2,1,0:T(8,128)S(1)} %fusion.8, f32[2,4,4,128,128]{4,3,2,1,0:T(8,128)S(1)} %fusion.159, f32[2,4,4,128,128]{4,3,2,1,0:T(8,128)S(1)} %fusion.30, f32[]{:T(128)S(6)} %mul.931), kind=kOutput, calls=%fused_computation.48 | convolution fusion | flops 807124992 | bytes 8388612 | tf_op jit(solution)/shard_map/transpose(jvp(...ab,kb->...ak))/dot_general | solution.py:45
  253.5 4.9 %fusion.104 = f32[2,4,4,128,64]{3,4,2,1,0:T(8,128)S(1)} fusion(f32[2,4,4,128,128]{3,4,2,1,0:T(8,128)} %copy.193, f32[2,4,4,128,128]{4,3,2,1,0:T(8,128)} %copy-done.7, f32[128,128]{0,1:T(8,128)S(1)} %sine_negate_fusion), kind=kOutput, calls=%fused_computation.126 | convolution fusion | flops 403701760 | bytes 5275648 | tf_op jit(solution)/shard_map/transpose(jvp(ja,...ak->...jk))/dot_general | solution.py:56
  268.0 4.4 fusion.38
  272.4 5.5 %fusion.97 = f32[4,4,64,64]{3,2,1,0:T(8,128)} fusion(f32[2,4,4,64,64]{4,3,2,1,0:T(8,128)S(1)} %fusion.38, f32[2,4,4,64,64]{4,3,2,1,0:T(8,128)S(1)} %fusion.347, f32[2,4,4,64,128]{4,3,2,1,0:T(8,128)S(1)} %fusion.91, f32[4,4,64,64]{3,2,1,0:T(8,128)S(1)} %mul.919, f32[64,64]{1,0:T(8,128)S(1)} %fusion.210, f32[2]{0:T(128)S(1)} %add_divide_fusion.6, ...), kind=kOutput, calls=%fused_computation.114 | convolution fusion | flops 202440704 | bytes 3998208 | tf_op jit(solution)/shard_map/transpose(jvp(...ab,kb->...ak))/dot_general | solution.py:47
  280.5 42.2 %all-reduce = f32[4,45,32]{1,0,2:T(4,128)S(1)} all-reduce(f32[4,45,32]{1,0,2:T(4,128)S(1)} %copy.194), channel_id=2, replica_groups=mesh['sub'=32] {'sub'}, use_global_device_ids=true, to_apply=%region_5.6.clone | all-reduce | flops 5760 | bytes 46080
  322.7 31.5 %all_gather.7 = f32[4,45,32]{1,0,2:T(4,128)S(1)} all-gather(f32[4,45,1]{1,0,2:T(4,128)S(1)} %fusion.212), channel_id=1, replica_groups=mesh['sub'=32] {'sub'}, dimensions={2}, use_global_device_ids=true | all-gather | bytes 23760 | tf_op jit(solution)/shard_map/all_gather | solution.py:114
  356.9 4.4 fusion.44
  361.3 5.1 %fusion.46 = f32[2,4,4,64,128]{4,3,2,1,0:T(8,128)S(1)} fusion(f32[4,4,64,64]{3,2,1,0:T(8,128)S(1)} %mul.967, f32[64,64]{1,0:T(8,128)S(1)} %fusion.210, f32[2]{0:T(128)S(1)} %add_divide_fusion.6, f32[128,128]{0,1:T(8,128)} %copy-done.11), kind=kOutput, calls=%fused_computation.80 | convolution fusion | flops 201588736 | bytes 1359880 | tf_op jit(solution)/shard_map/jvp(...ab,kb->...ak)/dot_general | solution.py:50
  366.4 4.7 fusion.69
  373.0 4.3 fusion.66
  423.0 4.2 fusion.42
  427.3 5.7 %fusion.96 = f32[4,4,64,64]{3,2,1,0:T(8,128)} fusion(f32[2,4,4,64,64]{4,3,2,1,0:T(8,128)S(1)} %fusion.42, f32[2,4,4,64,64]{4,3,2,1,0:T(8,128)S(1)} %fusion.344, f32[2,4,4,64,128]{4,3,2,1,0:T(8,128)S(1)} %fusion.87, f32[4,4,64,64]{3,2,1,0:T(8,128)S(1)} %mul.967, f32[64,64]{1,0:T(8,128)S(1)} %fusion.210, f32[2]{0:T(128)S(1)} %add_divide_fusion.6, ...), kind=kOutput, calls=%fused_computation.113 | convolution fusion | flops 202440704 | bytes 3998208 | tf_op jit(solution)/shard_map/transpose(jvp(...ab,kb->...ak))/dot_general | solution.py:47
  435.6 49.2 %all-reduce.1 = f32[4,45,32]{1,0,2:T(4,128)S(1)} all-reduce(f32[4,45,32]{1,0,2:T(4,128)S(1)} %copy.224), channel_id=3, replica_groups=mesh['sub'=32] {'sub'}, use_global_device_ids=true, to_apply=%region_10.11.clone | all-reduce | flops 5760 | bytes 46080
  (123 shorter events, 143.1 us)
Async XLA Ops:
  0.6 106.8 %copy-start = (f32[45,4096]{1,0:T(8,128)S(1)}, f32[45,4096]{1,0:T(8,128)}, u32[]{:S(2)}) copy-start(f32[45,4096]{1,0:T(8,128)} %param.9) | copy-start | bytes 2211844
  30.1 6.1 %copy-start.15 = (f32[4,45,1]{1,2,0:T(1,128)S(1)}, f32[4,45,1]{1,2,0:T(1,128)}, u32[]{:S(2)}) copy-start(f32[4,45,1]{1,2,0:T(1,128)} %param.8) | copy-start | bytes 2164
  30.1 77.1 %copy-start.16 = (s32[4]{0:T(128)S(1)}, s32[4]{0:T(128)}, u32[]{:S(2)}) copy-start(s32[4]{0:T(128)} %param.7) | copy-start | bytes 52
  30.1 118.2 %all-to-all-start = ((f32[32,1,16384]{2,1,0:T(1,128)}), f32[32,1,16384]{2,1,0:T(1,128)}, u32[]{:S(2)}, u32[]{:S(2)}) async-start(f32[32,1,16384]{2,1,0:T(1,128)} %reshape.149), calls=%async_computation | async-start | bytes 4194304 | tf_op jit(solution)/shard_map/all_to_all | solution.py:68
  36.2 74.0 %copy-start.17 = (s32[4]{0:T(128)S(1)}, s32[4]{0:T(128)}, u32[]{:S(2)}) copy-start(s32[4]{0:T(128)} %param.6) | copy-start | bytes 52
  110.2 22.0 %copy-start.11 = (f32[128,128]{0,1:T(8,128)}, f32[128,128]{0,1:T(8,128)S(1)}, u32[]{:S(2)}) copy-start(f32[128,128]{0,1:T(8,128)S(1)} %fusion.194) | copy-start | bytes 196612
  139.5 61.6 %copy-start.4 = (f32[2,4,4,128,128]{4,3,2,1,0:T(8,128)}, f32[2,4,4,128,128]{4,3,2,1,0:T(8,128)S(1)}, u32[]{:S(2)}) copy-start(f32[2,4,4,128,128]{4,3,2,1,0:T(8,128)S(1)} %convolution_subtract_fusion.1) | copy-start | bytes 6291460
  143.0 1.3 copy-start.7
  186.0 26.8 %collective-permute-start = (f32[2,4,512,128]{3,2,1,0:T(8,128)}, f32[2,4,512,128]{3,2,1,0:T(8,128)}, u32[]{:S(2)}, u32[]{:S(2)}) collective-permute-start(f32[2,4,512,128]{3,2,1,0:T(8,128)} %bitcast.274), channel_id=1, source_target_pairs={{1,0},{2,1},{3,2},{4,3},{5,4},{6,5},{7,6},{8,7},{9,8},{10,9},{11,1... | collective-permute-start | bytes 6291464 | tf_op jit(solution)/shard_map/ppermute | solution.py:19
  197.3 3.8 copy-start.8
  205.7 2.1 copy-start.10
  207.7 2.1 copy-start.6
  215.5 1.7 copy-start.14
  231.1 2.0 copy-start.2
  253.4 4.9 %copy-start.1 = (f32[2,4,4,128,128]{3,4,2,1,0:T(8,128)S(1)}, f32[2,4,4,128,128]{3,4,2,1,0:T(8,128)}, u32[]{:S(2)}) copy-start(f32[2,4,4,128,128]{3,4,2,1,0:T(8,128)} %copy.193) | copy-start | bytes 6291460
  253.4 4.9 %copy-start.9 = (f32[2,4,4,128,128]{4,3,2,1,0:T(8,128)S(1)}, f32[2,4,4,128,128]{4,3,2,1,0:T(8,128)}, u32[]{:S(2)}) copy-start(f32[2,4,4,128,128]{4,3,2,1,0:T(8,128)} %copy-done.7) | copy-start | bytes 6291460
  253.4 4.9 %copy-start.12 = (f32[128,128]{0,1:T(8,128)S(1)}, f32[128,128]{0,1:T(8,128)}, u32[]{:S(2)}) copy-start(f32[128,128]{0,1:T(8,128)} %copy-done.11) | copy-start | bytes 196612
  258.4 2.5 copy-start.5
  356.9 9.5 %copy-start.13 = (f32[128,128]{0,1:T(8,128)S(1)}, f32[128,128]{0,1:T(8,128)}, u32[]{:S(2)}) copy-start(f32[128,128]{0,1:T(8,128)} %copy-done.11) | copy-start | bytes 196612
  392.2 2.3 copy-start.3
where the time goes:
time: 490 us; the launch traced here: 486 us
  blocking collectives  194 us (40%)
  matrix products  182 us (37%)
  local copies, waits for them, and re-layouts  70 us (14%)
  other arithmetic  18.1 us (4%)
  between operations  9.91 us (2%)
  starting transfers between devices  9.19 us (2%)
    all_gather x2, blocking collectives, on_device(): gathered = lax.all_gather(current, 'sub', axis=2, tiled=True)  102 us
    unnamed x2, blocking collectives  91.4 us
    unnamed x39, local copies, waits for them, and re-layouts  45.6 us
    dot_general x9, matrix products, complex_dft(): jnp.einsum('...ab,kb->...ak', real_part, right_real, precision=highest)  32.6 us
    dot_general x9, matrix products, complex_dft(): jnp.einsum('...ab,kb->...ak', real_part, right_imag, precision=highest)  28.1 us
    dot_general x9, matrix products, complex_dft(): jnp.einsum('ja,...ak->...jk', left_imag, half_real, precision=highest)  22.5 us
    dot_general x9, matrix products, complex_dft(): jnp.einsum('ja,...ak->...jk', left_real, half_imag, precision=highest)  21.8 us
    dot_general x9, matrix products, complex_dft(): jnp.einsum('ja,...ak->...jk', left_imag, half_imag, precision=highest)  21.1 us
  transfers between devices with their start and end apart: 2, of which 1 were waited for; matrix products, arithmetic and copies ran while one was open for 11% of the time, Pallas kernels for 0%

commit v1 on v0

--- a/solution.py
+++ b/solution.py
@@ -11,6 +11,23 @@
 PUP = 64
 GAMMA = 0.01
 STEP_SIZE = 0.05
+
+
+def laid_out(tiles, dim):
+    tiles = jnp.moveaxis(tiles, 0, dim)
+    shape = tiles.shape
+    return tiles.reshape(*shape[:dim], shape[dim] * shape[dim + 1], *shape[dim + 2 :])
+
+
+def grow_blocks(x, axis):
+    devices, mine = (lax.axis_size(axis), lax.axis_index(axis))
+    blocks, bit = (x[None], 1)
+    while bit < devices:
+        other = lax.ppermute(blocks, axis, [(i, i ^ bit) for i in range(devices)])
+        low = mine & bit == 0
+        blocks = jnp.concatenate([jnp.where(low, blocks, other), jnp.where(low, other, blocks)])
+        bit *= 2
+    return blocks
 
 
 def from_behind(block, axis, distance):
@@ -111,7 +128,7 @@
     current = coeffs
     gradient = jnp.zeros_like(coeffs)
     for iteration in range(ITERS):
-        gathered = lax.all_gather(current, "sub", axis=2, tiled=True)
+        gathered = laid_out(grow_blocks(current, "sub"), 2)
         chosen = jnp.einsum("fmp,ps->fms", gathered, selector, precision=highest)
         loss_value, pullback = jax.vjp(objective, chosen)
         (slopes,) = pullback(jnp.ones_like(loss_value))

time: 490 us -> 435 us (0.89)
  blocking collectives: 194 us -> 83.9 us
  waiting for transfers between devices: 2.58 us -> 50.2 us
  starting transfers between devices: 9.19 us -> 20 us
    all_gather x2 -> x0, blocking collectives: 102 us -> none  [on_device(): gathered = lax.all_gather(current, 'sub', axis=2, tiled=True)]
    ppermute x0 -> x10, waiting for transfers between devices: none -> 42 us  [grow_blocks(): other = lax.ppermute(blocks, axis, [(i, i ^ bit) for i in range(devices)])]
    ppermute x0 -> x10, starting transfers between devices: none -> 11.2 us  [grow_blocks(): other = lax.ppermute(blocks, axis, [(i, i ^ bit) for i in range(devices)])]
    unnamed x2, blocking collectives: 91.4 us -> 83.9 us
    ppermute x1, waiting for transfers between devices: 2.58 us -> 8.17 us  [from_behind(): return lax.ppermute(block, axis, route)]
    unnamed x39 -> x35, local copies, waits for them, and re-layouts: 45.6 us -> 44.5 us
  transfers between devices with their start and end apart: 2 -> 12, of which waited for: 1 -> 10; matrix products, arithmetic and copies ran while one was open for 11% -> 12% of each run, Pallas kernels for 0% -> 0%
where the time goes in v1:
time: 435 us; the launch traced here: 429 us
  matrix products  181 us (42%)
  blocking collectives  83.9 us (19%)
  local copies, waits for them, and re-layouts  66.5 us (15%)
  waiting for transfers between devices  50.2 us (12%)
  starting transfers between devices  20 us (5%)
  other arithmetic  16.9 us (4%)
  between operations  9.97 us (2%)
    unnamed x2, blocking collectives  83.9 us
    unnamed x35, local copies, waits for them, and re-layouts  44.5 us
    ppermute x10, waiting for transfers between devices, grow_blocks(): other = lax.ppermute(blocks, axis, [(i, i ^ bit) for i in range(devices)])  42 us
    dot_general x9, matrix products, complex_dft(): jnp.einsum('...ab,kb->...ak', real_part, right_real, precision=highest)  32.6 us
    dot_general x9, matrix products, complex_dft(): jnp.einsum('...ab,kb->...ak', real_part, right_imag, precision=highest)  28.3 us
    dot_general x9, matrix products, complex_dft(): jnp.einsum('ja,...ak->...jk', left_imag, half_real, precision=highest)  24.1 us
    dot_general x9, matrix products, complex_dft(): jnp.einsum('ja,...ak->...jk', left_imag, half_imag, precision=highest)  21.1 us
    dot_general x9, matrix products, complex_dft(): jnp.einsum('ja,...ak->...jk', left_real, half_real, precision=highest)  20.2 us
  transfers between devices with their start and end apart: 12, of which 10 were waited for; matrix products, arithmetic and copies ran while one was open for 12% of the time, Pallas kernels for 0%

profile of v1, /device:TPU:10, one launch (start us, length us, event | category | flops | bytes accessed | tf_op | source)
XLA Modules:
  0.0 428.9 jit_solution(5118168849451816080)
XLA Ops:
  0.6 13.2 %copy.175 = f32[2,4,16,4096]{2,1,0,3:T(4,128)} copy(f32[2,4,16,4096]{3,2,1,0:T(8,128)} %param.5) | data formatting | bytes 4194304 | tf_op args[0]
  13.8 16.4 %reshape.157 = f32[32,1,16384]{2,1,0:T(1,128)} reshape(f32[4096,2,4,16]{3,2,1,0:T(4,128)} %bitcast.284) | data formatting | bytes 4194304
  30.2 6.2 %all-to-all-start = ((f32[32,1,16384]{2,1,0:T(1,128)}), f32[32,1,16384]{2,1,0:T(1,128)}, u32[]{:S(2)}, u32[]{:S(2)}) async-start(f32[32,1,16384]{2,1,0:T(1,128)} %reshape.157), calls=%async_computation | async-start | bytes 4194304 | tf_op jit(solution)/shard_map/all_to_all | solution.py:85
  38.8 9.4 %collective-permute-done.1 = f32[2,4,45,1]{2,0,1,3:T(2,128)S(1)} collective-permute-done((f32[2,4,45,1]{2,0,1,3:T(2,128)S(1)}, f32[2,4,45,1]{2,0,1,3:T(2,128)S(1)}, u32[]{:S(2)}, u32[]{:S(2)}) %collective-permute-start.1) | collective-permute-done | bytes 1472 | tf_op jit(solution)/shard_map/ppermute | solution.py:26
  55.7 16.4 %collective-permute-done.3 = f32[8,4,45,1]{2,0,1,3:T(8,128)S(1)} collective-permute-done((f32[8,4,45,1]{2,0,1,3:T(8,128)S(1)}, f32[8,4,45,1]{2,0,1,3:T(8,128)S(1)}, u32[]{:S(2)}, u32[]{:S(2)}) %collective-permute-start.3) | collective-permute-done | bytes 5792 | tf_op jit(solution)/shard_map/ppermute | solution.py:26
  84.3 4.4 %fusion.52 = f32[2,4,4,64,128]{4,3,2,1,0:T(8,128)S(1)} fusion(f32[4,4,64,64]{3,2,1,0:T(8,128)S(1)} %mul.919, f32[64,64]{1,0:T(8,128)S(1)} %fusion.213, f32[2]{0:T(128)S(1)} %add_divide_fusion.6, f32[128,128]{0,1:T(8,128)S(1)} %sine_negate_fusion), kind=kOutput, calls=%fused_computation.83 | convolution fusion | flops 201588736 | bytes 1638912 | tf_op jit(solution)/shard_map/jvp(...ab,kb->...ak)/dot_general | solution.py:64
  88.7 4.4 %fusion.54 = f32[2,4,4,64,128]{4,3,2,1,0:T(8,128)S(1)} fusion(f32[4,4,64,64]{3,2,1,0:T(8,128)S(1)} %mul.919, f32[64,64]{1,0:T(8,128)S(1)} %fusion.213, f32[2]{0:T(128)S(1)} %add_divide_fusion.6, f32[128,128]{0,1:T(8,128)S(1)} %fusion.197), kind=kOutput, calls=%fused_computation.84 | convolution fusion | flops 201588736 | bytes 1638912 | tf_op jit(solution)/shard_map/jvp(...ab,kb->...ak)/dot_general | solution.py:67
  93.1 4.6 %fusion.63 = f32[2,4,4,64,128]{4,3,2,1,0:T(8,128)S(1)} fusion(f32[2,4,4,64,128]{4,3,2,1,0:T(8,128)S(1)} %fusion.52, f32[4,4,64,64]{3,2,1,0:T(8,128)S(1)} %mul.919, f32[64,64]{1,0:T(8,128)S(1)} %fusion.213, f32[2]{0:T(128)S(1)} %add_divide_fusion.6, f32[128,128]{0,1:T(8,128)S(1)} %fusion.197), kind=kOutput, calls=%fused_computation.88 | convolution fusion | flops 201850880 | bytes 2687488 | tf_op jit(solution)/shard_map/jvp(...ab,kb->...ak)/dot_general | solution.py:61
  97.7 4.4 %fusion.60 = f32[2,4,4,64,128]{4,3,2,1,0:T(8,128)S(1)} fusion(f32[2,4,4,64,128]{4,3,2,1,0:T(8,128)S(1)} %fusion.54, f32[4,4,64,64]{3,2,1,0:T(8,128)S(1)} %mul.919, f32[64,64]{1,0:T(8,128)S(1)} %fusion.213, f32[2]{0:T(128)S(1)} %add_divide_fusion.6, f32[128,128]{0,1:T(8,128)S(1)} %sine_negate_fusion), kind=kOutput, calls=%fused_computation.87 | convolution fusion | flops 201850880 | bytes 2687488 | tf_op jit(solution)/shard_map/jvp(...ab,kb->...ak)/dot_general | solution.py:62
  113.0 4.8 %convolution_add_fusion.1 = f32[2,4,4,128,128]{4,3,2,1,0:T(8,128)} fusion(f32[2,4,4,128,128]{4,3,2,1,0:T(8,128)S(1)} %fusion.354, f32[2,4,4,64,128]{4,3,2,1,0:T(8,128)S(1)} %fusion.63, f32[128,128]{0,1:T(8,128)S(1)} %sine_negate_fusion), kind=kOutput, calls=%fused_computation.60 | convolution fusion | flops 403177472 | bytes 5275648 | tf_op jit(solution)/shard_map/jvp(ja,...ak->...jk)/dot_general | solution.py:73
  118.3 8.9 %reduce.6 = f32[32,16384]{1,0:T(8,128)} reduce(f32[32,1,16384]{2,1,0:T(1,128)} %all-to-all-done, f32[]{:T(128)} %broadcast.349), dimensions={1}, to_apply=%all_to_all.13.reduce_sub_computation | reduce | bytes 4194308 | tf_op jit(solution)/shard_map/all_to_all | solution.py:85
  127.2 14.7 %reshape.158 = f32[4096,2,4,16]{3,2,1,0:T(4,128)} reshape(f32[32,16384]{1,0:T(8,128)} %reduce.6) | data formatting | bytes 4194304
  141.9 13.7 %copy.288 = f32[2,4,16,32,128]{4,2,3,1,0:T(8,128)} copy(f32[2,4,16,32,128]{2,1,0,4,3:T(4,128)} %bitcast.283) | data formatting | bytes 4194304 | tf_op jit(solution)/shard_map/all_to_all | solution.py:85
  173.8 8.2 %collective-permute-done.5 = f32[2,4,512,128]{3,2,1,0:T(8,128)S(1)} collective-permute-done((f32[2,4,512,128]{3,2,1,0:T(8,128)}, f32[2,4,512,128]{3,2,1,0:T(8,128)S(1)}, u32[]{:S(2)}, u32[]{:S(2)}) %collective-permute-start.5) | collective-permute-done | bytes 2097184 | tf_op jit(solution)/shard_map/ppermute | solution.py:36
  211.5 4.9 %add_divide_fusion.2 = f32[2,4,4,128,128]{4,3,2,1,0:T(8,128)} fusion(f32[2,4,4,128,128]{4,3,2,1,0:T(8,128)S(1)} %fusion.8, f32[2,4,4,128,128]{4,3,2,1,0:T(8,128)S(1)} %fusion.165, f32[2,4,4,128,128]{4,3,2,1,0:T(8,128)S(1)} %fusion.30, f32[]{:T(128)S(6)} %mul.931), kind=kOutput, calls=%fused_computation.48 | convolution fusion | flops 807124992 | bytes 8388612 | tf_op jit(solution)/shard_map/transpose(jvp(...ab,kb->...ak))/dot_general | solution.py:62
  219.9 4.9 %fusion.104 = f32[2,4,4,128,64]{3,4,2,1,0:T(8,128)S(1)} fusion(f32[2,4,4,128,128]{3,4,2,1,0:T(8,128)} %copy.196, f32[2,4,4,128,128]{4,3,2,1,0:T(8,128)} %convolution_add_fusion.1, f32[128,128]{0,1:T(8,128)S(1)} %sine_negate_fusion), kind=kOutput, calls=%fused_computation.125 | convolution fusion | flops 403701760 | bytes 5275648 | tf_op jit(solution)/shard_map/transpose(jvp(ja,...ak->...jk))/dot_general | solution.py:73
  234.4 4.4 %fusion.38 = f32[2,4,4,64,64]{4,3,2,1,0:T(8,128)S(1)} fusion(f32[2,4,4,64,64]{4,3,2,1,0:T(8,128)S(1)} %fusion.348, f32[2,4,4,64,128]{4,3,2,1,0:T(8,128)S(1)} %fusion.91, f32[4,4,64,64]{3,2,1,0:T(8,128)S(1)} %mul.919, f32[64,64]{1,0:T(8,128)S(1)} %fusion.213, f32[2]{0:T(128)S(1)} %add_divide_fusion.6, f32[128,128]{0,1:T(8,128)S(1)} %copy-done.10), kind=kOutput, calls=%fused_computation.73 | convolution fusion | flops 201981952 | bytes 3211776 | tf_op jit(solution)/shard_map/transpose(jvp(...ab,kb->...ak))/dot_general | solution.py:61
  238.8 5.6 %fusion.97 = f32[4,4,64,64]{3,2,1,0:T(8,128)} fusion(f32[2,4,4,64,64]{4,3,2,1,0:T(8,128)S(1)} %fusion.38, f32[2,4,4,64,64]{4,3,2,1,0:T(8,128)S(1)} %fusion.352, f32[2,4,4,64,128]{4,3,2,1,0:T(8,128)S(1)} %fusion.91, f32[4,4,64,64]{3,2,1,0:T(8,128)S(1)} %mul.919, f32[64,64]{1,0:T(8,128)S(1)} %fusion.213, f32[2]{0:T(128)S(1)} %add_divide_fusion.6, ...), kind=kOutput, calls=%fused_computation.114 | convolution fusion | flops 202440704 | bytes 3998208 | tf_op jit(solution)/shard_map/transpose(jvp(...ab,kb->...ak))/dot_general | solution.py:64
  246.9 43.8 %all-reduce = f32[4,45,32]{1,0,2:T(4,128)S(1)} all-reduce(f32[4,45,32]{1,0,2:T(4,128)S(1)} %copy.197), channel_id=2, replica_groups=mesh['sub'=32] {'sub'}, use_global_device_ids=true, to_apply=%region_5.6.clone | all-reduce | flops 5760 | bytes 46080
  311.0 4.4 %fusion.44 = f32[2,4,4,64,128]{4,3,2,1,0:T(8,128)S(1)} fusion(f32[4,4,64,64]{3,2,1,0:T(8,128)S(1)} %mul.967, f32[64,64]{1,0:T(8,128)S(1)} %fusion.213, f32[2]{0:T(128)S(1)} %add_divide_fusion.6, f32[128,128]{0,1:T(8,128)S(1)} %sine_negate_fusion), kind=kOutput, calls=%fused_computation.79 | convolution fusion | flops 201588736 | bytes 1638912 | tf_op jit(solution)/shard_map/jvp(...ab,kb->...ak)/dot_general | solution.py:64
  315.4 5.1 %fusion.46 = f32[2,4,4,64,128]{4,3,2,1,0:T(8,128)S(1)} fusion(f32[4,4,64,64]{3,2,1,0:T(8,128)S(1)} %mul.967, f32[64,64]{1,0:T(8,128)S(1)} %fusion.213, f32[2]{0:T(128)S(1)} %add_divide_fusion.6, f32[128,128]{0,1:T(8,128)} %copy-done.9), kind=kOutput, calls=%fused_computation.80 | convolution fusion | flops 201588736 | bytes 1359880 | tf_op jit(solution)/shard_map/jvp(...ab,kb->...ak)/dot_general | solution.py:67
  320.6 4.7 %fusion.69 = f32[2,4,4,64,128]{4,3,2,1,0:T(8,128)S(1)} fusion(f32[2,4,4,64,128]{4,3,2,1,0:T(8,128)S(1)} %fusion.44, f32[4,4,64,64]{3,2,1,0:T(8,128)S(1)} %mul.967, f32[64,64]{1,0:T(8,128)S(1)} %fusion.213, f32[2]{0:T(128)S(1)} %add_divide_fusion.6, f32[128,128]{0,1:T(8,128)S(1)} %copy-done.11), kind=kOutput, calls=%fused_computation.90 | convolution fusion | flops 201850880 | bytes 2687488 | tf_op jit(solution)/shard_map/jvp(...ab,kb->...ak)/dot_general | solution.py:61
  381.7 4.7 %fusion.96 = f32[4,4,64,64]{3,2,1,0:T(8,128)S(1)} fusion(f32[2,4,4,64,64]{4,3,2,1,0:T(8,128)S(1)} %fusion.42, f32[2,4,4,64,64]{4,3,2,1,0:T(8,128)S(1)} %fusion.349, f32[2,4,4,64,128]{4,3,2,1,0:T(8,128)S(1)} %fusion.87, f32[4,4,64,64]{3,2,1,0:T(8,128)S(1)} %mul.967, f32[64,64]{1,0:T(8,128)S(1)} %fusion.213, f32[2]{0:T(128)S(1)} %add_divide_fusion.6, ...), kind=kOutput, calls=%fused_computation.113 | convolution fusion | flops 202440704 | bytes 3998208 | tf_op jit(solution)/shard_map/transpose(jvp(...ab,kb->...ak))/dot_general | solution.py:64
  387.9 40.1 %all-reduce.1 = f32[4,45,32]{1,0,2:T(4,128)S(1)} all-reduce(f32[4,45,32]{1,0,2:T(4,128)S(1)} %copy.226), channel_id=3, replica_groups=mesh['sub'=32] {'sub'}, use_global_device_ids=true, to_apply=%region_10.11.clone | all-reduce | flops 5760 | bytes 46080
  (155 shorter events, 166.6 us)
Async XLA Ops:
  0.6 82.9 %copy-start = (f32[45,4096]{1,0:T(8,128)S(1)}, f32[45,4096]{1,0:T(8,128)}, u32[]{:S(2)}) copy-start(f32[45,4096]{1,0:T(8,128)} %param.9) | copy-start | bytes 2211844
  30.2 6.3 %copy-start.13 = (f32[4,45,1]{1,2,0:T(1,128)S(1)}, f32[4,45,1]{1,2,0:T(1,128)}, u32[]{:S(2)}) copy-start(f32[4,45,1]{1,2,0:T(1,128)} %param.8) | copy-start | bytes 2164
  30.2 7.3 %copy-start.15 = (s32[4]{0:T(128)S(1)}, s32[4]{0:T(128)}, u32[]{:S(2)}) copy-start(s32[4]{0:T(128)} %param.6) | copy-start | bytes 52
  30.2 53.1 %copy-start.14 = (s32[4]{0:T(128)S(1)}, s32[4]{0:T(128)}, u32[]{:S(2)}) copy-start(s32[4]{0:T(128)} %param.7) | copy-start | bytes 52
  30.2 87.6 %all-to-all-start = ((f32[32,1,16384]{2,1,0:T(1,128)}), f32[32,1,16384]{2,1,0:T(1,128)}, u32[]{:S(2)}, u32[]{:S(2)}) async-start(f32[32,1,16384]{2,1,0:T(1,128)} %reshape.157), calls=%async_computation | async-start | bytes 4194304 | tf_op jit(solution)/shard_map/all_to_all | solution.py:85
  36.5 1.3 collective-permute-start
  37.8 10.3 %collective-permute-start.1 = (f32[2,4,45,1]{2,0,1,3:T(2,128)S(1)}, f32[2,4,45,1]{2,0,1,3:T(2,128)S(1)}, u32[]{:S(2)}, u32[]{:S(2)}) collective-permute-start(f32[2,4,45,1]{2,0,1,3:T(2,128)S(1)} %pad_maximum_fusion.6), channel_id=1, source_target_pairs={{0,2},{1,3},{2,0},{3,1},{4,6},{5,7},{6,4},{7,5},{8,10},{9,11},{10,... | collective-permute-start | bytes 4328 | tf_op jit(solution)/shard_map/ppermute | solution.py:26
  38.7 66.8 %copy-start.9 = (f32[128,128]{0,1:T(8,128)}, f32[128,128]{0,1:T(8,128)S(1)}, u32[]{:S(2)}) copy-start(f32[128,128]{0,1:T(8,128)S(1)} %fusion.197) | copy-start | bytes 196612
  48.2 3.7 collective-permute-start.2
  52.0 20.1 %collective-permute-start.3 = (f32[8,4,45,1]{2,0,1,3:T(8,128)S(1)}, f32[8,4,45,1]{2,0,1,3:T(8,128)S(1)}, u32[]{:S(2)}, u32[]{:S(2)}) collective-permute-start(f32[8,4,45,1]{2,0,1,3:T(8,128)S(1)} %pad_maximum_fusion.2), channel_id=1, source_target_pairs={{0,8},{1,9},{2,10},{3,11},{4,12},{5,13},{6,14},{7,15},{8,0},{9,1},... | collective-permute-start | bytes 17288 | tf_op jit(solution)/shard_map/ppermute | solution.py:26
  72.1 11.2 %collective-permute-start.4 = (f32[16,4,45,1]{2,0,1,3:T(8,128)S(1)}, f32[16,4,45,1]{2,0,1,3:T(8,128)S(1)}, u32[]{:S(2)}, u32[]{:S(2)}) collective-permute-start(f32[16,4,45,1]{2,0,1,3:T(8,128)S(1)} %pad_maximum_fusion), channel_id=1, source_target_pairs={{0,16},{1,17},{2,18},{3,19},{4,20},{5,21},{6,22},{7,23},{8,24},{9,... | collective-permute-start | bytes 34568 | tf_op jit(solution)/shard_map/ppermute | solution.py:26
  112.9 51.3 %copy-start.4 = (f32[2,4,4,128,128]{4,3,2,1,0:T(8,128)}, f32[2,4,4,128,128]{4,3,2,1,0:T(8,128)S(1)}, u32[]{:S(2)}) copy-start(f32[2,4,4,128,128]{4,3,2,1,0:T(8,128)S(1)} %convolution_subtract_fusion.1) | copy-start | bytes 6291460
  155.6 26.4 %collective-permute-start.5 = (f32[2,4,512,128]{3,2,1,0:T(8,128)}, f32[2,4,512,128]{3,2,1,0:T(8,128)S(1)}, u32[]{:S(2)}, u32[]{:S(2)}) collective-permute-start(f32[2,4,512,128]{3,2,1,0:T(8,128)} %bitcast.285), channel_id=1, source_target_pairs={{1,0},{2,1},{3,2},{4,3},{5,4},{6,5},{7,6},{8,7},{9,8},{10,9},{11,1... | collective-permute-start | bytes 6291464 | tf_op jit(solution)/shard_map/ppermute | solution.py:36
  170.9 2.5 copy-start.6
  219.8 4.9 %copy-start.1 = (f32[2,4,4,128,128]{3,4,2,1,0:T(8,128)S(1)}, f32[2,4,4,128,128]{3,4,2,1,0:T(8,128)}, u32[]{:S(2)}) copy-start(f32[2,4,4,128,128]{3,4,2,1,0:T(8,128)} %copy.196) | copy-start | bytes 6291460
  219.8 4.9 %copy-start.8 = (f32[2,4,4,128,128]{4,3,2,1,0:T(8,128)S(1)}, f32[2,4,4,128,128]{4,3,2,1,0:T(8,128)}, u32[]{:S(2)}) copy-start(f32[2,4,4,128,128]{4,3,2,1,0:T(8,128)} %convolution_add_fusion.1) | copy-start | bytes 6291460
  219.8 4.9 %copy-start.10 = (f32[128,128]{0,1:T(8,128)S(1)}, f32[128,128]{0,1:T(8,128)}, u32[]{:S(2)}) copy-start(f32[128,128]{0,1:T(8,128)} %copy-done.9) | copy-start | bytes 196612
  224.8 2.5 copy-start.5
  290.8 1.2 collective-permute-start.6
  292.0 3.7 collective-permute-start.7
  295.7 3.7 collective-permute-start.8
  299.5 4.0 collective-permute-start.9
  303.5 4.9 %collective-permute-start.10 = (f32[16,4,45,1]{2,0,1,3:T(8,128)S(1)}, f32[16,4,45,1]{2,0,1,3:T(8,128)S(1)}, u32[]{:S(2)}, u32[]{:S(2)}) collective-permute-start(f32[16,4,45,1]{2,0,1,3:T(8,128)S(1)} %pad_maximum_fusion.1), channel_id=1, source_target_pairs={{0,16},{1,17},{2,18},{3,19},{4,20},{5,21},{6,22},{7,23},{8,24},{9,... | collective-permute-start | bytes 34568 | tf_op jit(solution)/shard_map/ppermute | solution.py:26
  311.0 9.5 %copy-start.11 = (f32[128,128]{0,1:T(8,128)S(1)}, f32[128,128]{0,1:T(8,128)}, u32[]{:S(2)}) copy-start(f32[128,128]{0,1:T(8,128)} %copy-done.9) | copy-start | bytes 196612
  (4 other events, 7.2 us)
